TPU v7x, 32 devices: a whole 2x2x4 slice. The times are simulated.
32 devices in a mesh: dp: 16 (over z, y, x), mp: 2 (over core).
Axes of the slice: x: 2, y: 2, z: 4, core: 2. Of those that a mesh axis runs over, the one named last changes fastest.
Arguments:
- head_out: bfloat16 [3, 2048, 4096], P(None, 'dp', 'mp'), may hold values from -6 to 6
- residual: bfloat16 [3, 2048, 4096], P(None, 'dp', 'mp'), may hold values from -6 to 6
- out_weight: bfloat16 [4096, 4096], P('dp', 'mp'), may hold values from -0.09375 to 0.09375
- strategy_table: bfloat16 [64, 4096], P(None, 'mp'), may hold values from -3 to 3
- meta_graph: int32 [64, 64], replicated, may hold values from 0 to 3, as said below
- strategy_ids: int32 [3, 2048], P(None, 'dp'), may hold values from 0 to 63
- cotangent: bfloat16 [3, 2048, 4096], P(None, 'dp', 'mp'), may hold values from -6 to 6
Outputs:
- layer_out: bfloat16 [3, 2048, 4096], P(None, 'dp', 'mp')
- head_grad: bfloat16 [3, 2048, 4096], P(None, 'dp', 'mp')
- weight_grad: float32 [4096, 4096], P('dp', 'mp')
- table_grad: float32 [64, 4096], P(None, 'mp')
Inputs may be any that keep to these rules, and one draw needn't show every extreme that they name: `meta_graph`: entries are zero on and above the diagonal; the last strategy meets the first with weight 3.
All inputs are finite; a program needn't handle non-finite values.
Results may differ from a plain program's by a relative error of at most 0.009.
Values may be sent and summed in bfloat16 or wider, within the bound.
A program may use at most 192 MiB of HBM per device.

v0:
```python
import math
import jax
import jax.numpy as jnp
from jax import lax
from jax.sharding import PartitionSpec as P


def mixture(meta_graph):
    counts = meta_graph.astype(jnp.float32)
    totals = jnp.maximum(jnp.sum(counts, axis=1, keepdims=True), 1.0)
    return jnp.eye(meta_graph.shape[0], dtype=jnp.float32) + counts / totals


def on_device(head_out, residual, out_weight, strategy_table, meta_graph, strategy_ids, cotangent):
    highest = lax.Precision.HIGHEST
    batches, local_rows, head_cols = head_out.shape
    strategies = meta_graph.shape[0]
    mixing = mixture(meta_graph)
    table = jnp.dot(mixing, strategy_table.astype(jnp.float32), precision=highest)
    grad_scale = 1.0 / math.sqrt(batches * local_rows * lax.axis_size("dp"))
    model_width = out_weight.shape[0] * lax.axis_size("dp")
    full_weight = lax.all_gather(out_weight, "dp", axis=0, tiled=True)
    weight_acc = jnp.zeros((model_width, head_cols), jnp.float32)
    table_acc = jnp.zeros(table.shape, jnp.float32)
    outputs = []
    head_grads = []
    for batch in range(batches):
        current = head_out[batch]
        partial_sum = lax.dot_general(
            current, full_weight, (((1,), (1,)), ((), ())), preferred_element_type=jnp.float32
        )
        projected = lax.psum_scatter(
            partial_sum.astype(jnp.bfloat16), "mp", scatter_dimension=1, tiled=True
        ).astype(jnp.float32)
        one_hot = (
            strategy_ids[batch][:, None] == lax.broadcasted_iota(jnp.int32, (1, strategies), 1)
        ).astype(jnp.float32)
        gating = 1.0 + jnp.dot(one_hot, table, precision=highest)
        outputs.append(
            (residual[batch].astype(jnp.float32) + projected * gating).astype(jnp.bfloat16)
        )
        grad_local = (cotangent[batch].astype(jnp.float32) * gating).astype(jnp.bfloat16)
        full_grad = lax.all_gather(grad_local, "mp", axis=1, tiled=True)
        head_grad = jnp.dot(full_grad, full_weight, preferred_element_type=jnp.float32)
        head_grads.append(head_grad.astype(jnp.bfloat16))
        cond_grad = cotangent[batch].astype(jnp.float32) * projected
        table_acc = table_acc + lax.dot_general(
            one_hot,
            cond_grad,
            (((0,), (0,)), ((), ())),
            precision=highest,
            preferred_element_type=jnp.float32,
        )
        if batch + 1 < batches:
            weight_acc = weight_acc + lax.dot_general(
                full_grad, current, (((0,), (0,)), ((), ())), preferred_element_type=jnp.float32
            )
    weight_acc = weight_acc + lax.dot_general(
        full_grad, current, (((0,), (0,)), ((), ())), preferred_element_type=jnp.float32
    )
    weight_sum = lax.psum_scatter(weight_acc, "dp", scatter_dimension=0, tiled=True)
    table_sum = lax.psum(table_acc, "dp")
    table_grad = jnp.dot(mixing.T, table_sum, precision=highest) * grad_scale
    return (jnp.stack(outputs), jnp.stack(head_grads), weight_sum * grad_scale, table_grad)


def solution(mesh):
    placed = (
        P(None, "dp", "mp"),
        P(None, "dp", "mp"),
        P("dp", "mp"),
        P(None, "mp"),
        P(),
        P(None, "dp"),
        P(None, "dp", "mp"),
    )
    return jax.shard_map(
        on_device,
        mesh=mesh,
        in_specs=placed,
        out_specs=(P(None, "dp", "mp"), P(None, "dp", "mp"), P("dp", "mp"), P(None, "mp")),
        check_vma=False,
    )
```

profile of v0, /device:TPU:10, one launch (start us, length us, event | category | flops | bytes accessed | tf_op | source)
XLA Modules:
  0.0 1102.9 jit_solution(4540015493611375227)
XLA Ops:
  7.2 0.0 copy-start
  7.2 0.0 all-gather.5.cloned.1.call-start
  7.2 0.7 all-gather.5.cloned.1.call-update
  7.9 0.0 copy-start.5
  7.9 0.0 reduce-scatter.9.cloned.1.call-start
  8.0 193.1 %all-gather.5.cloned.1.call-done = bf16[4096,2048]{1,0:T(8,128)(2,1)} async-done(((bf16[256,2048]{1,0:T(8,128)(2,1)}), bf16[4096,2048]{1,0:T(8,128)(2,1)}) %all-gather.5.cloned.1.call-update) | async-done | bytes 16777232 | tf_op jit(solution)/shard_map/all_gather | solution.py:22
  201.1 12.6 %convolution_convert_fusion = bf16[128,4096]{1,0:T(8,128)(2,1)} fusion(bf16[4096,2048]{1,0:T(8,128)(2,1)} %all-gather.5.cloned.1.call-done, bf16[3,128,2048]{2,1,0:T(8,128)(2,1)} %param.7), kind=kOutput, calls=%fused_computation.1 | convolution fusion | flops 2148007936 | bytes 18350080 | tf_op jit(solution)/shard_map/dot_general | solution.py:29
  213.6 0.0 reduce-scatter.9.cloned.1.call-update
  213.7 0.0 reduce-scatter.7.cloned.1.call-start
  213.7 0.0 copy-done.5
  213.7 12.4 %convolution_convert_fusion.1 = bf16[128,4096]{1,0:T(8,128)(2,1)} fusion(bf16[4096,2048]{1,0:T(8,128)(2,1)} %all-gather.5.cloned.1.call-done, bf16[3,128,2048]{2,1,0:T(8,128)(2,1)S(1)} %copy-done.5), kind=kOutput, calls=%fused_computation.2 | convolution fusion | flops 2148007936 | bytes 18350080 | tf_op jit(solution)/shard_map/dot_general | solution.py:29
  226.1 0.0 reduce-scatter.7.cloned.1.call-update
  226.1 0.0 copy-start.11
  226.1 0.0 copy-start.12
  226.1 0.0 reduce-scatter.5.cloned.1.call-start
  226.2 12.4 %convolution_convert_fusion.2 = bf16[128,4096]{1,0:T(8,128)(2,1)} fusion(bf16[4096,2048]{1,0:T(8,128)(2,1)} %all-gather.5.cloned.1.call-done, bf16[3,128,2048]{2,1,0:T(8,128)(2,1)S(1)} %copy-done.5), kind=kOutput, calls=%fused_computation.3 | convolution fusion | flops 2148007936 | bytes 18350080 | tf_op jit(solution)/shard_map/dot_general | solution.py:29
  238.6 0.0 reduce-scatter.5.cloned.1.call-update
  238.6 0.2 all-gather.9.cloned.1.call-start
  238.8 0.0 copy-done.11
  238.8 0.1 convert_reduce_fusion
  238.9 0.0 copy-done.12
  239.0 0.0 copy-done
  239.0 0.4 fusion.42
  239.4 0.6 convolution_add_fusion
  240.0 1.6 convolution_add_fusion.1
  241.6 6.3 reduce-scatter.5.cloned.1.call-done
  247.9 5.1 fusion.15
  253.0 0.0 all-gather.9.cloned.1.call-update
  253.1 0.0 all-gather.7.cloned.1.call-start
  253.1 0.5 all-gather.7.cloned.1.call-update
  253.7 0.0 all-gather.11.cloned.1.call-start
  253.7 0.0 copy-start.6
  253.7 0.7 all-gather.11.cloned.1.call-update
  254.4 0.0 all-reduce.2.cloned.1.call-start
  254.4 1.9 fusion.10
  256.3 0.0 copy-done.7
  256.3 1.7 convolution_add_fusion.4
  258.0 0.0 copy-done.6
  258.1 2.5 convolution_add_fusion.3
  260.6 0.0 all-reduce.2.cloned.1.call-update
  260.6 0.0 reduce-scatter.11.cloned.1.call-start
  260.6 2.8 all-gather.9.cloned.1.call-done
  263.4 15.0 %fusion.21 = f32[4096,2048]{1,0:T(8,128)} fusion(bf16[128,4096]{1,0:T(8,128)(2,1)} %all-gather.9.cloned.1.call-done, bf16[3,128,2048]{2,1,0:T(8,128)(2,1)S(1)} %copy-done.5), kind=kOutput, calls=%fused_computation.46 | convolution fusion | flops 2147483648 | bytes 35127296 | tf_op jit(solution)/shard_map/dot_general | solution.py:55
  278.4 14.7 %fusion.24 = f32[4096,2048]{1,0:T(8,128)} fusion(bf16[128,4096]{1,0:T(8,128)(2,1)} %all-gather.7.cloned.1.call-done, bf16[3,128,2048]{2,1,0:T(8,128)(2,1)S(1)} %copy-done.5), kind=kOutput, calls=%fused_computation.49 | convolution fusion | flops 2147483648 | bytes 35127296 | tf_op jit(solution)/shard_map/dot_general | solution.py:55
  293.1 34.7 %add_add_fusion = f32[4096,2048]{1,0:T(8,128)} fusion(f32[4096,2048]{1,0:T(8,128)} %fusion.24, f32[4096,2048]{1,0:T(8,128)} %fusion.21, bf16[128,4096]{1,0:T(8,128)(2,1)} %all-gather.11.cloned.1.call-done, bf16[3,128,2048]{2,1,0:T(8,128)(2,1)S(1)} %copy-done.5), kind=kOutput, calls=%fused_computation | convolution fusion | flops 2164260864 | bytes 102236160 | tf_op jit(solution)/shard_map/dot_general | solution.py:58
  327.9 0.0 reduce-scatter.11.cloned.1.call-update
  327.9 1.0 copy-done.8
  328.9 0.2 copy-done.9
  329.1 0.2 copy-done.10
  329.2 1.3 pad_maximum_fusion
  330.5 71.3 %all-reduce.2.cloned.1.call-done = f32[64,2048]{1,0:T(8,128)} async-done(((f32[64,2048]{1,0:T(8,128)}), f32[64,2048]{1,0:T(8,128)}) %all-reduce.2.cloned.1.call-update) | async-done | bytes 524304 | tf_op jit(solution)/shard_map/psum | solution.py:62
  401.9 2.5 convolution_multiply_fusion
  404.4 0.0 copy-done.3
  404.4 0.0 slice-start.2
  404.4 8.3 fusion
  412.7 0.0 copy-done.4
  412.8 0.0 slice-start.3
  412.8 0.0 copy-start.2
  412.8 9.0 fusion.2
  421.9 2.5 fusion.1
  424.4 0.0 copy-start.1
  424.4 1.3 pad_maximum_fusion.1
  425.7 667.4 %reduce-scatter.11.cloned.1.call-done = f32[256,2048]{1,0:T(8,128)} async-done(((f32[4096,2048]{1,0:T(8,128)}), f32[256,2048]{1,0:T(8,128)}) %reduce-scatter.11.cloned.1.call-update) | async-done | bytes 2097168 | tf_op jit(solution)/shard_map/reduce_scatter | solution.py:61
  1093.1 3.2 broadcast_multiply_fusion
  (21 shorter events, 0.0 us)
Async XLA Ops:
  7.2 231.8 %copy-start = (bf16[64,2048]{1,0:T(8,128)(2,1)S(1)}, bf16[64,2048]{1,0:T(8,128)(2,1)}, u32[]{:S(2)}) copy-start(bf16[64,2048]{1,0:T(8,128)(2,1)} %param.10) | copy-start | bytes 786436
  7.2 193.9 %all-gather.5.cloned.1.call-start = ((), (), s32[]{:S(2)}) async-start(), calls=%async_computation.4 | async-start | bytes 17825792 | tf_op jit(solution)/shard_map/all_gather | solution.py:22
  7.9 205.8 %copy-start.5 = (bf16[3,128,2048]{2,1,0:T(8,128)(2,1)S(1)}, bf16[3,128,2048]{2,1,0:T(8,128)(2,1)}, u32[]{:S(2)}) copy-start(bf16[3,128,2048]{2,1,0:T(8,128)(2,1)} %param.7) | copy-start | bytes 4718596
  7.9 233.7 %reduce-scatter.9.cloned.1.call-start = ((), (), s32[]{:S(2)}) async-start(), calls=%async_computation.7 | async-start | bytes 1572864 | tf_op jit(solution)/shard_map/reduce_scatter | solution.py:32
  213.7 28.0 %reduce-scatter.7.cloned.1.call-start = ((), (), s32[]{:S(2)}) async-start(), calls=%async_computation.6 | async-start | bytes 1572864 | tf_op jit(solution)/shard_map/reduce_scatter | solution.py:32
  226.1 12.7 %copy-start.11 = (s32[64,64]{1,0:T(8,128)S(1)}, s32[64,64]{1,0:T(8,128)}, u32[]{:S(2)}) copy-start(s32[64,64]{1,0:T(8,128)} %param.11) | copy-start | bytes 49156
  226.1 12.8 %copy-start.12 = (s32[3,128]{1,0:T(4,128)S(1)}, s32[3,128]{1,0:T(4,128)}, u32[]{:S(2)}) copy-start(s32[3,128]{1,0:T(4,128)} %param.12) | copy-start | bytes 4612
  226.1 21.8 %reduce-scatter.5.cloned.1.call-start = ((), (), s32[]{:S(2)}) async-start(), calls=%async_computation.5 | async-start | bytes 1572864 | tf_op jit(solution)/shard_map/reduce_scatter | solution.py:32
  238.6 24.8 %all-gather.9.cloned.1.call-start = ((), (), s32[]{:S(2)}) async-start(), calls=%async_computation.9 | async-start | bytes 1572864 | tf_op jit(solution)/shard_map/all_gather | solution.py:43
  253.0 3.3 copy-start.7
  253.1 25.3 %all-gather.7.cloned.1.call-start = ((), (), s32[]{:S(2)}) async-start(), calls=%async_computation.8 | async-start | bytes 1572864 | tf_op jit(solution)/shard_map/all_gather | solution.py:43
  253.7 39.5 %all-gather.11.cloned.1.call-start = ((), (), s32[]{:S(2)}) async-start(), calls=%async_computation.10 | async-start | bytes 1572864 | tf_op jit(solution)/shard_map/all_gather | solution.py:43
  253.7 4.3 copy-start.6
  254.4 147.5 %all-reduce.2.cloned.1.call-start = ((), (), s32[]{:S(2)}) async-start(), calls=%async_computation.12 | async-start | bytes 1048576 | tf_op jit(solution)/shard_map/psum | solution.py:62
  260.6 832.5 %reduce-scatter.11.cloned.1.call-start = ((), (), s32[]{:S(2)}) async-start(), calls=%async_computation.11 | async-start | bytes 35651584 | tf_op jit(solution)/shard_map/reduce_scatter | solution.py:61
  327.9 1.0 copy-start.8
  327.9 1.2 copy-start.9
  327.9 1.4 copy-start.10
  329.2 75.2 %copy-start.3 = (bf16[128,4096]{1,0:T(8,128)(2,1)S(1)}, bf16[128,4096]{1,0:T(8,128)(2,1)}, u32[]{:S(2)}) copy-start(bf16[128,4096]{1,0:T(8,128)(2,1)} %all-gather.7.cloned.1.call-done) | copy-start | bytes 3145732
  404.4 8.3 copy-start.4
  404.4 17.4 %slice-start = ((s8[16777216]{0:T(1024)(128)(4,1)}), s8[4194304]{0:T(1024)(128)(4,1)S(1)}, s32[]{:S(2)}) async-start(s8[16777216]{0:T(1024)(128)(4,1)} %bitcast.80), calls=%async_computation.13 | async-start | bytes 8388608
  404.4 17.4 %slice-start.1 = ((s8[16777216]{0:T(1024)(128)(4,1)}), s8[4194304]{0:T(1024)(128)(4,1)S(1)}, s32[]{:S(2)}) async-start(s8[16777216]{0:T(1024)(128)(4,1)} %bitcast.80), calls=%async_computation.14 | async-start | bytes 8388608
  404.4 17.4 %slice-start.2 = ((s8[16777216]{0:T(1024)(128)(4,1)}), s8[4194304]{0:T(1024)(128)(4,1)S(1)}, s32[]{:S(2)}) async-start(s8[16777216]{0:T(1024)(128)(4,1)} %bitcast.80), calls=%async_computation.15 | async-start | bytes 8388608
  412.8 9.1 slice-start.3
  412.8 9.1 copy-start.2
  424.4 672.0 %copy-start.1 = (bf16[64,2048]{1,0:T(8,128)(2,1)S(1)}, bf16[64,2048]{1,0:T(8,128)(2,1)}, u32[]{:S(2)}) copy-start(bf16[64,2048]{1,0:T(8,128)(2,1)} %param.10) | copy-start | bytes 786436
Sparse Core Ops, SparseCore 0:
  10.8 190.2 all-gather.4
  213.8 8.7 reduce-scatter.8
  226.2 8.9 reduce-scatter.6
  238.7 9.1 reduce-scatter.4
  253.2 10.1 all-gather.8
  264.8 10.1 all-gather.6
  276.6 10.1 all-gather.10
  292.5 109.2 all-reduce.1
  404.2 688.8 reduce-scatter.10
where the time goes:
time: 1100 us
  waiting for transfers between devices  943 us (86%)
  matrix products  138 us (13%)
  between operations  14.1 us (1%)
    reduce_scatter x1, waiting for transfers between devices, on_device(): lax.psum_scatter(weight_acc, 'dp', scatter_dimension=0, tiled=True)  667 us
    all_gather x1, waiting for transfers between devices, on_device(): full_weight = lax.all_gather(out_weight, 'dp', axis=0, tiled=True)  193 us
    psum x1, waiting for transfers between devices, on_device(): table_sum = lax.psum(table_acc, 'dp')  71.3 us
    dot_general x3, matrix products, on_device(): lax.dot_general(full_grad, current, (((0,), (0,)), ((), ())), preferred_e...  64.4 us
    dot_general x3, matrix products, on_device(): lax.dot_general(current, full_weight, (((1,), (1,)), ((), ())), preferred...  37.3 us
  transfers between devices with their start and end apart: 9, of which 5 were waited for; matrix products, arithmetic and copies ran while one was open for 11% of the time, Pallas kernels for 0%

commit v1 on v0

--- a/solution.py
+++ b/solution.py
@@ -19,7 +19,9 @@
     table = jnp.dot(mixing, strategy_table.astype(jnp.float32), precision=highest)
     grad_scale = 1.0 / math.sqrt(batches * local_rows * lax.axis_size("dp"))
     model_width = out_weight.shape[0] * lax.axis_size("dp")
-    full_weight = lax.all_gather(out_weight, "dp", axis=0, tiled=True)
+    full_weight = jnp.concatenate(
+        lax.all_to_all(jnp.stack([out_weight] * lax.axis_size("dp")), "dp", 0, 0), axis=0
+    )
     weight_acc = jnp.zeros((model_width, head_cols), jnp.float32)
     table_acc = jnp.zeros(table.shape, jnp.float32)
     outputs = []

time: 1100 us -> 1280 us (1.16)
  blocking collectives: 0 us -> 369 us
  waiting for transfers between devices: 943 us -> 748 us
    all_to_all x0 -> x1, blocking collectives: none -> 369 us  [on_device(): lax.all_to_all(jnp.stack([out_weight] * lax.axis_size('dp')), 'dp', 0, 0)]
    all_gather x1 -> x0, waiting for transfers between devices: 193 us -> none  [on_device(): full_weight = lax.all_gather(out_weight, 'dp', axis=0, tiled=True)]
  transfers between devices with their start and end apart: 9 -> 8, of which waited for: 5 -> 4; matrix products, arithmetic and copies ran while one was open for 11% -> 10% of each run, Pallas kernels for 0% -> 0%
where the time goes in v1:
time: 1280 us
  waiting for transfers between devices  748 us (58%)
  blocking collectives  369 us (29%)
  matrix products  138 us (11%)
  between operations  14.4 us (1%)
    reduce_scatter x1, waiting for transfers between devices, on_device(): lax.psum_scatter(weight_acc, 'dp', scatter_dimension=0, tiled=True)  667 us
    all_to_all x1, blocking collectives, on_device(): lax.all_to_all(jnp.stack([out_weight] * lax.axis_size('dp')), 'dp', 0, 0)  369 us
    psum x1, waiting for transfers between devices, on_device(): table_sum = lax.psum(table_acc, 'dp')  71.3 us
    dot_general x3, matrix products, on_device(): lax.dot_general(full_grad, current, (((0,), (0,)), ((), ())), preferred_e...  64.3 us
    dot_general x3, matrix products, on_device(): lax.dot_general(current, full_weight, (((1,), (1,)), ((), ())), preferred...  37.3 us
  transfers between devices with their start and end apart: 8, of which 4 were waited for; matrix products, arithmetic and copies ran while one was open for 10% of the time, Pallas kernels for 0%

profile of v1, /device:TPU:10, one launch (start us, length us, event | category | flops | bytes accessed | tf_op | source)
XLA Modules:
  0.0 1281.0 jit_solution(14918082927766021620)
XLA Ops:
  7.2 0.0 copy-start
  7.2 0.0 reduce-scatter.9.cloned.1.call-start
  7.2 3.9 stack.18
  11.1 0.0 copy-start.5
  11.1 369.1 %all_to_all.5 = bf16[16,256,2048]{2,1,0:T(8,128)(2,1)} all-to-all(bf16[16,256,2048]{2,1,0:T(8,128)(2,1)S(1)} %stack.18), channel_id=1, replica_groups=mesh['dp'=16,'mp'=2] {'dp'}, dimensions={0} | all-to-all | bytes 33554432 | tf_op jit(solution)/shard_map/all_to_all | solution.py:23
  380.2 0.0 copy-done.5
  380.2 12.4 convolution_convert_fusion
  392.6 0.0 reduce-scatter.9.cloned.1.call-update
  392.6 0.0 reduce-scatter.7.cloned.1.call-start
  392.7 12.4 convolution_convert_fusion.1
  405.1 0.0 reduce-scatter.7.cloned.1.call-update
  405.1 0.0 copy-start.11
  405.1 0.0 copy-start.12
  405.1 0.2 reduce-scatter.5.cloned.1.call-start
  405.3 12.5 convolution_convert_fusion.2
  417.8 0.0 reduce-scatter.5.cloned.1.call-update
  417.9 0.0 all-gather.6.cloned.1.call-start
  417.9 0.0 copy-done.11
  417.9 0.1 convert_reduce_fusion
  418.0 0.0 copy-done.12
  418.1 0.0 copy-done
  418.1 0.4 fusion.42
  418.5 0.6 convolution_add_fusion
  419.1 1.6 convolution_add_fusion.1
  420.7 5.2 reduce-scatter.5.cloned.1.call-done
  425.9 5.1 fusion.15
  431.1 0.0 all-gather.6.cloned.1.call-update
  431.1 0.0 all-gather.4.cloned.1.call-start
  431.1 0.5 all-gather.4.cloned.1.call-update
  431.7 0.0 all-gather.8.cloned.1.call-start
  431.7 0.0 copy-start.6
  431.7 0.5 all-gather.8.cloned.1.call-update
  432.3 0.0 all-reduce.2.cloned.1.call-start
  432.3 1.9 fusion.10
  434.2 0.0 copy-done.7
  434.2 1.7 convolution_add_fusion.4
  435.9 0.0 copy-done.6
  435.9 2.5 convolution_add_fusion.3
  438.4 0.0 all-reduce.2.cloned.1.call-update
  438.4 0.3 reduce-scatter.11.cloned.1.call-start
  438.7 2.7 all-gather.6.cloned.1.call-done
  441.4 14.8 %fusion.21 = f32[4096,2048]{1,0:T(8,128)} fusion(bf16[128,4096]{1,0:T(8,128)(2,1)} %all-gather.6.cloned.1.call-done, bf16[3,128,2048]{2,1,0:T(8,128)(2,1)S(1)} %copy-done.5), kind=kOutput, calls=%fused_computation.46 | convolution fusion | flops 2147483648 | bytes 35127296 | tf_op jit(solution)/shard_map/dot_general | solution.py:57
  456.3 14.7 %fusion.24 = f32[4096,2048]{1,0:T(8,128)} fusion(bf16[128,4096]{1,0:T(8,128)(2,1)} %all-gather.4.cloned.1.call-done, bf16[3,128,2048]{2,1,0:T(8,128)(2,1)S(1)} %copy-done.5), kind=kOutput, calls=%fused_computation.49 | convolution fusion | flops 2147483648 | bytes 35127296 | tf_op jit(solution)/shard_map/dot_general | solution.py:57
  471.0 34.8 %add_add_fusion = f32[4096,2048]{1,0:T(8,128)} fusion(f32[4096,2048]{1,0:T(8,128)} %fusion.24, f32[4096,2048]{1,0:T(8,128)} %fusion.21, bf16[128,4096]{1,0:T(8,128)(2,1)} %all-gather.8.cloned.1.call-done, bf16[3,128,2048]{2,1,0:T(8,128)(2,1)S(1)} %copy-done.5), kind=kOutput, calls=%fused_computation | convolution fusion | flops 2164260864 | bytes 102236160 | tf_op jit(solution)/shard_map/dot_general | solution.py:60
  505.7 0.0 reduce-scatter.11.cloned.1.call-update
  505.8 1.0 copy-done.8
  506.8 0.2 copy-done.9
  506.9 0.2 copy-done.10
  507.1 1.3 pad_maximum_fusion
  508.4 71.3 %all-reduce.2.cloned.1.call-done = f32[64,2048]{1,0:T(8,128)} async-done(((f32[64,2048]{1,0:T(8,128)}), f32[64,2048]{1,0:T(8,128)}) %all-reduce.2.cloned.1.call-update) | async-done | bytes 524304 | tf_op jit(solution)/shard_map/psum | solution.py:64
  579.8 2.5 convolution_multiply_fusion
  582.3 0.0 copy-done.3
  582.3 0.0 slice-start.2
  582.3 8.3 fusion
  590.6 0.0 copy-done.4
  590.6 0.0 slice-start.3
  590.6 0.0 copy-start.2
  590.7 9.0 fusion.2
  599.7 2.5 fusion.1
  602.2 0.0 copy-start.1
  602.3 1.3 pad_maximum_fusion.1
  603.6 667.4 %reduce-scatter.11.cloned.1.call-done = f32[256,2048]{1,0:T(8,128)} async-done(((f32[4096,2048]{1,0:T(8,128)}), f32[256,2048]{1,0:T(8,128)}) %reduce-scatter.11.cloned.1.call-update) | async-done | bytes 2097168 | tf_op jit(solution)/shard_map/reduce_scatter | solution.py:63
  1271.0 3.2 broadcast_multiply_fusion
  1274.2 0.0 copy-done.1
  (20 shorter events, 0.0 us)
Async XLA Ops:
  7.2 410.9 %copy-start = (bf16[64,2048]{1,0:T(8,128)(2,1)S(1)}, bf16[64,2048]{1,0:T(8,128)(2,1)}, u32[]{:S(2)}) copy-start(bf16[64,2048]{1,0:T(8,128)(2,1)} %param.10) | copy-start | bytes 786436
  7.2 413.6 %reduce-scatter.9.cloned.1.call-start = ((), (), s32[]{:S(2)}) async-start(), calls=%async_computation.7 | async-start | bytes 1572864 | tf_op jit(solution)/shard_map/reduce_scatter | solution.py:34
  11.1 369.1 %copy-start.5 = (bf16[3,128,2048]{2,1,0:T(8,128)(2,1)S(1)}, bf16[3,128,2048]{2,1,0:T(8,128)(2,1)}, u32[]{:S(2)}) copy-start(bf16[3,128,2048]{2,1,0:T(8,128)(2,1)} %param.7) | copy-start | bytes 4718596
  392.6 28.1 %reduce-scatter.7.cloned.1.call-start = ((), (), s32[]{:S(2)}) async-start(), calls=%async_computation.6 | async-start | bytes 1572864 | tf_op jit(solution)/shard_map/reduce_scatter | solution.py:34
  405.1 12.8 %copy-start.11 = (s32[64,64]{1,0:T(8,128)S(1)}, s32[64,64]{1,0:T(8,128)}, u32[]{:S(2)}) copy-start(s32[64,64]{1,0:T(8,128)} %param.11) | copy-start | bytes 49156
  405.1 12.9 %copy-start.12 = (s32[3,128]{1,0:T(4,128)S(1)}, s32[3,128]{1,0:T(4,128)}, u32[]{:S(2)}) copy-start(s32[3,128]{1,0:T(4,128)} %param.12) | copy-start | bytes 4612
  405.1 20.8 %reduce-scatter.5.cloned.1.call-start = ((), (), s32[]{:S(2)}) async-start(), calls=%async_computation.5 | async-start | bytes 1572864 | tf_op jit(solution)/shard_map/reduce_scatter | solution.py:34
  417.9 23.6 %all-gather.6.cloned.1.call-start = ((), (), s32[]{:S(2)}) async-start(), calls=%async_computation.9 | async-start | bytes 1572864 | tf_op jit(solution)/shard_map/all_gather | solution.py:45
  431.1 3.1 copy-start.7
  431.1 25.2 %all-gather.4.cloned.1.call-start = ((), (), s32[]{:S(2)}) async-start(), calls=%async_computation.8 | async-start | bytes 1572864 | tf_op jit(solution)/shard_map/all_gather | solution.py:45
  431.7 39.3 %all-gather.8.cloned.1.call-start = ((), (), s32[]{:S(2)}) async-start(), calls=%async_computation.10 | async-start | bytes 1572864 | tf_op jit(solution)/shard_map/all_gather | solution.py:45
  431.7 4.2 copy-start.6
  432.3 147.5 %all-reduce.2.cloned.1.call-start = ((), (), s32[]{:S(2)}) async-start(), calls=%async_computation.12 | async-start | bytes 1048576 | tf_op jit(solution)/shard_map/psum | solution.py:64
  438.4 832.5 %reduce-scatter.11.cloned.1.call-start = ((), (), s32[]{:S(2)}) async-start(), calls=%async_computation.11 | async-start | bytes 35651584 | tf_op jit(solution)/shard_map/reduce_scatter | solution.py:63
  505.7 1.0 copy-start.8
  505.7 1.2 copy-start.9
  505.7 1.4 copy-start.10
  507.1 75.2 %copy-start.3 = (bf16[128,4096]{1,0:T(8,128)(2,1)S(1)}, bf16[128,4096]{1,0:T(8,128)(2,1)}, u32[]{:S(2)}) copy-start(bf16[128,4096]{1,0:T(8,128)(2,1)} %all-gather.4.cloned.1.call-done) | copy-start | bytes 3145732
  582.3 8.3 copy-start.4
  582.3 17.4 %slice-start = ((s8[16777216]{0:T(1024)(128)(4,1)}), s8[4194304]{0:T(1024)(128)(4,1)S(1)}, s32[]{:S(2)}) async-start(s8[16777216]{0:T(1024)(128)(4,1)} %bitcast.86), calls=%async_computation.13 | async-start | bytes 8388608
  582.3 17.4 %slice-start.1 = ((s8[16777216]{0:T(1024)(128)(4,1)}), s8[4194304]{0:T(1024)(128)(4,1)S(1)}, s32[]{:S(2)}) async-start(s8[16777216]{0:T(1024)(128)(4,1)} %bitcast.86), calls=%async_computation.14 | async-start | bytes 8388608
  582.3 17.4 %slice-start.2 = ((s8[16777216]{0:T(1024)(128)(4,1)}), s8[4194304]{0:T(1024)(128)(4,1)S(1)}, s32[]{:S(2)}) async-start(s8[16777216]{0:T(1024)(128)(4,1)} %bitcast.86), calls=%async_computation.15 | async-start | bytes 8388608
  590.6 9.1 slice-start.3
  590.6 9.1 copy-start.2
  602.2 671.9 %copy-start.1 = (bf16[64,2048]{1,0:T(8,128)(2,1)S(1)}, bf16[64,2048]{1,0:T(8,128)(2,1)}, u32[]{:S(2)}) copy-start(bf16[64,2048]{1,0:T(8,128)(2,1)} %param.10) | copy-start | bytes 786436
Sparse Core Ops, SparseCore 0:
  392.7 8.0 reduce-scatter.8
  405.2 8.0 reduce-scatter.6
  418.0 7.9 reduce-scatter.4
  431.2 10.1 all-gather.5
  442.8 10.1 all-gather.3
  454.5 10.1 all-gather.7
  470.4 109.2 all-reduce.1
  582.1 688.8 reduce-scatter.10
